TPU v7x, 512 devices: a whole 4x4x16 slice. The times are simulated.
512 devices in a mesh: group: 64 (over z, y_hi, core), tp: 8 (over x, y_lo).
Axes of the slice: x: 4, y: 4 (y_hi: 2, y_lo: 2; y = y_hi * 2 + y_lo), z: 16, core: 2. Of those that a mesh axis runs over, the one named last changes fastest.
Arguments:
- queries: bfloat16 [4096, 2048], P('group', 'tp'), may hold values from -22 to 22
- new_kv: bfloat16 [4096, 1024], P('group', 'tp'), may hold values from -6 to 6
- local_cache: bfloat16 [16384, 1024], P('group', 'tp'), may hold values from -6 to 6
- remote_pool: bfloat16 [32768, 1024], P('group', 'tp'), may hold values from -6 to 6
- page_index: int32 [64, 64], P('group'), may hold values from 0 to 63, each once within a row
- lengths: int32 [64], P('group'), may hold values from 256 to 768, as said below
- sinks: float32 [32], P('tp'), may hold values from 4 to 8
- out_weight: bfloat16 [2048, 2880], P('tp'), may hold values from -0.125 to 0.125
- residual: bfloat16 [4096, 2880], P('group', 'tp'), may hold values from -6 to 6
- norm_gain: float32 [2880], replicated, may hold values from 0.5 to 2
- routes: int32 [4096, 4], P('group'), may hold values from 0 to 31, all different within a row; in each aligned block of 64 rows (0 to 63, 64 to 127, ...) at most 10 rows name the same one
- route_weights: float32 [4096, 4], P('group'), may hold values from 0.1 to 1
- expert_gate: bfloat16 [64, 2880, 1440], P('group', None, 'tp'), may hold values from -0.109375 to 0.109375
- expert_up: bfloat16 [64, 2880, 1440], P('group', None, 'tp'), may hold values from -0.109375 to 0.109375
- expert_down: bfloat16 [64, 1440, 2880], P('group', None, 'tp'), may hold values from -0.109375 to 0.109375
Outputs:
- layer_out: bfloat16 [4096, 2880], P('group', 'tp')
Inputs may be any that keep to these rules, and one draw needn't show every extreme that they name: `lengths`: every request has at least 256 cached positions; some request has exactly 256, some exactly 768. `routes`: within the rows of one request no expert is named by more than 10 rows. `page_index`: each row is a permutation.
All inputs are finite; a program needn't handle non-finite values.
Results may differ from a plain program's by a relative error of at most 0.013.
Values may be sent and summed in bfloat16 or wider, within the bound.
A program may use at most 64 MiB of HBM per device.

v0:
```python
import jax
import jax.numpy as jnp
from jax import lax
from jax.sharding import PartitionSpec as P

HEAD = 64
THETA = 150000.0
ALPHA = 1.702
EPSILON = 1e-05


def rotate(values, positions):
    half_dim = values.shape[-1] // 2
    inverse = THETA ** (-2.0 * jnp.arange(half_dim, dtype=jnp.float32) / values.shape[-1])
    angles = positions[:, None, None] * inverse[None, None, :]
    cosine = jnp.cos(angles)
    sine_part = jnp.sin(angles)
    first_part = values[..., :half_dim]
    second_part = values[..., half_dim:]
    return jnp.concatenate(
        [
            first_part * cosine - second_part * sine_part,
            second_part * cosine + first_part * sine_part,
        ],
        axis=-1,
    )


def attend(query_rows, kv_rows, cache_kv, cache_valid, sinks, length):
    block_len = query_rows.shape[0]
    kv_heads = kv_rows.shape[1] // (2 * HEAD)
    query_heads = query_rows.shape[1] // HEAD
    group_size = query_heads // kv_heads
    positions = (length + jnp.arange(block_len, dtype=jnp.int32)).astype(jnp.float32)
    query_rot = rotate(
        query_rows.astype(jnp.float32).reshape(block_len, query_heads, HEAD), positions
    ).astype(jnp.bfloat16)
    kv_parts = kv_rows.reshape(block_len, kv_heads, 2, HEAD)
    key_rot = rotate(kv_parts[:, :, 0].astype(jnp.float32), positions).astype(jnp.bfloat16)
    cache_parts = cache_kv.reshape(cache_kv.shape[0], kv_heads, 2, HEAD)
    all_keys = jnp.concatenate([cache_parts[:, :, 0], key_rot], axis=0)
    all_values = jnp.concatenate([cache_parts[:, :, 1], kv_parts[:, :, 1]], axis=0)
    token_order = jnp.arange(block_len, dtype=jnp.int32)
    causal = token_order[None, :] <= token_order[:, None]
    allowed = jnp.concatenate(
        [jnp.broadcast_to(cache_valid[None, :], (block_len, cache_valid.shape[0])), causal], axis=1
    )
    row_allowed = jnp.repeat(allowed, group_size, axis=0)
    score_scale = HEAD ** (-0.5)
    query_block = query_rot.reshape(block_len * group_size, HEAD)
    scores = (
        jnp.dot(query_block, all_keys[:, 0].T, preferred_element_type=jnp.float32) * score_scale
    )
    scores = jnp.where(row_allowed, scores, -jnp.inf)
    sink_rows = jnp.tile(sinks, block_len)
    row_max = jnp.maximum(jnp.max(scores, axis=1), sink_rows)
    weights = jnp.exp(scores - row_max[:, None])
    denominator = jnp.sum(weights, axis=1) + jnp.exp(sink_rows - row_max)
    blended = (
        jnp.dot(weights.astype(jnp.bfloat16), all_values[:, 0], preferred_element_type=jnp.float32)
        / denominator[:, None]
    )
    outputs = blended.astype(jnp.bfloat16).reshape(block_len, group_size * HEAD)
    return outputs


def on_device(
    queries,
    new_kv,
    local_cache,
    remote_pool,
    page_index,
    lengths,
    sinks,
    out_weight,
    residual,
    norm_gain,
    routes,
    route_weights,
    expert_gate,
    expert_up,
    expert_down,
):
    groups = lax.axis_size("group")
    lane_count = remote_pool.shape[1]
    local_len = local_cache.shape[0]
    fetched = lax.all_to_all(
        remote_pool.reshape(groups, -1, lane_count),
        "group",
        split_axis=0,
        concat_axis=0,
        tiled=True,
    )
    page_len = fetched.shape[1]
    length = lengths[0]
    offsets = jnp.arange(page_len, dtype=jnp.int32)
    remote_pos = local_len + page_index[0][:, None] * page_len + offsets[None, :]
    cache_valid = jnp.concatenate(
        [jnp.ones((local_len,), jnp.bool_), (remote_pos < length).reshape(-1)]
    )
    cache_kv = jnp.concatenate([local_cache, fetched.reshape(-1, lane_count)], axis=0)
    attended = attend(queries, new_kv, cache_kv, cache_valid, sinks, length)
    width = residual.shape[1]
    start = lax.axis_index("tp") * width
    own_gain = lax.dynamic_slice_in_dim(norm_gain, start, width, 0)
    partial_sum = jnp.dot(attended, out_weight, preferred_element_type=jnp.float32)
    own_cols = lax.dynamic_slice_in_dim(partial_sum, start, width, 1) + residual.astype(jnp.float32)
    partial_sum = lax.dynamic_update_slice_in_dim(partial_sum, own_cols, start, 1)
    hidden_state = lax.psum(partial_sum, "tp")
    mean_square = jnp.mean(hidden_state * hidden_state, axis=1, keepdims=True)
    own_state = lax.dynamic_slice_in_dim(hidden_state, start, width, 1)
    normed_own = (own_state * lax.rsqrt(mean_square + EPSILON) * own_gain).astype(jnp.bfloat16)
    block_len = normed_own.shape[0]
    top_count = routes.shape[1]
    experts = groups // 2
    capacity = 5 * block_len * top_count // (4 * experts)
    member = jnp.any(
        routes[:, :, None] == jnp.arange(experts, dtype=jnp.int32)[None, None, :], axis=1
    ).astype(jnp.int32)
    slot_rank = jnp.cumsum(member, axis=0) - member
    slot_hit = member[:, :, None] * (
        slot_rank[:, :, None] == jnp.arange(capacity, dtype=jnp.int32)[None, None, :]
    ).astype(jnp.int32)
    slot_token = jnp.sum(slot_hit * jnp.arange(block_len, dtype=jnp.int32)[:, None, None], axis=0)
    slot_valid = jnp.sum(slot_hit, axis=0)
    send_own = jnp.take(normed_own, slot_token.reshape(-1), axis=0) * slot_valid.reshape(
        -1, 1
    ).astype(jnp.bfloat16)
    hidden_part = expert_gate.shape[2]
    gate_and_up = jnp.concatenate([expert_gate[0], expert_up[0]], axis=1)
    outgoing = send_own
    feature_count = outgoing.shape[1]
    outgoing = outgoing.reshape(experts, 1, capacity, feature_count)
    outgoing = jnp.broadcast_to(outgoing, (experts, 2, capacity, feature_count)).reshape(
        groups, capacity, feature_count
    )
    whole = lax.all_gather(
        lax.all_to_all(outgoing, "group", split_axis=0, concat_axis=0, tiled=True),
        "tp",
        axis=2,
        tiled=True,
    )
    sources, slot_count, features = whole.shape
    flat_rows = whole.reshape(sources * slot_count, features)
    both = jnp.dot(flat_rows, gate_and_up, preferred_element_type=jnp.float32)
    gate_val = both[:, :hidden_part]
    up_val = both[:, hidden_part:]
    active = (gate_val * jax.nn.sigmoid(ALPHA * gate_val) * (up_val + 1.0)).astype(jnp.bfloat16)
    joined = lax.all_gather(active, "tp", axis=1, tiled=True)
    result = jnp.dot(joined, expert_down[0], preferred_element_type=jnp.float32).astype(
        jnp.bfloat16
    )
    returned = result.reshape(sources, slot_count, result.shape[1])
    arrived = lax.all_to_all(returned, "group", split_axis=0, concat_axis=0, tiled=True)
    halves = arrived.reshape(experts, 2, capacity, width).astype(jnp.float32)
    summed = (halves[:, 0] + halves[:, 1]).reshape(experts * capacity, width)
    rank_at = jnp.take_along_axis(slot_rank, routes, axis=1)
    picked = jnp.take(summed, (routes * capacity + rank_at).reshape(-1), axis=0).reshape(
        block_len, top_count, width
    )
    mixing = route_weights / jnp.sum(route_weights, axis=1, keepdims=True)
    moe_out = jnp.sum(mixing[:, :, None] * picked, axis=1)
    return (own_state + moe_out).astype(jnp.bfloat16)


def solution(mesh):
    return jax.shard_map(
        on_device,
        mesh=mesh,
        in_specs=(
            P("group", "tp"),
            P("group", "tp"),
            P("group", "tp"),
            P("group", "tp"),
            P("group", None),
            P("group"),
            P("tp"),
            P("tp", None),
            P("group", "tp"),
            P(),
            P("group", None),
            P("group", None),
            P("group", None, "tp"),
            P("group", None, "tp"),
            P("group", None, "tp"),
        ),
        out_specs=P("group", "tp"),
        check_vma=False,
    )
```

profile of v0, /device:TPU:2, one launch (start us, length us, event | category | flops | bytes accessed | tf_op | source)
XLA Modules:
  0.0 590.5 jit_solution(3634151493439080288)
XLA Ops:
  6.5 18.9 %all-to-all-start = ((bf16[64,8,128]{2,1,0:T(8,128)(2,1)}), bf16[64,8,128]{2,1,0:T(8,128)(2,1)S(1)}, u32[]{:S(2)}, u32[]{:S(2)}) async-start(bf16[64,8,128]{2,1,0:T(8,128)(2,1)} %bitcast.65), calls=%async_computation | async-start | bytes 262144 | tf_op jit(solution)/shard_map/all_to_all | solution.py:87
  27.9 0.9 copy.144
  32.4 11.6 %all-to-all-done = bf16[64,8,128]{2,1,0:T(8,128)(2,1)S(1)} async-done(((bf16[64,8,128]{2,1,0:T(8,128)(2,1)}), bf16[64,8,128]{2,1,0:T(8,128)(2,1)S(1)}, u32[]{:S(2)}, u32[]{:S(2)}) %all-to-all-start) | async-done | bytes 131104 | tf_op jit(solution)/shard_map/all_to_all | solution.py:87
  47.3 1.1 dynamic_update_slice.3
  50.3 78.5 %all-reduce.3.cloned.1.call-done = f32[64,2880]{1,0:T(8,128)} async-done(((f32[64,2880]{1,0:T(8,128)}), f32[64,2880]{1,0:T(8,128)}) %all-reduce.3.cloned.1.call-update) | async-done | bytes 737296 | tf_op jit(solution)/shard_map/psum | solution.py:109
  128.8 1.3 multiply_reduce_fusion
  130.1 1.0 multiply_convert_fusion
  131.1 2.0 gather_fusion
  133.6 59.9 %all_to_all.15 = bf16[64,10,360]{2,1,0:T(8,128)(2,1)S(1)} all-to-all(bf16[64,10,360]{2,1,0:T(8,128)(2,1)S(1)} %bitcast.58), channel_id=1, replica_groups=mesh['group'=64,'tp'=8] {'group'}, dimensions={0} | all-to-all | bytes 921600 | tf_op jit(solution)/shard_map/all_to_all | solution.py:138
  193.5 2.0 copy.165
  195.8 231.1 %all-gather.4.cloned.1.call-done = bf16[64,10,2880]{0,1,2:T(8,128)(2,1)} async-done(((bf16[64,10,360]{0,1,2:T(8,128)(2,1)}), bf16[64,10,2880]{0,1,2:T(8,128)(2,1)}) %all-gather.4.cloned.1.call-update) | async-done | bytes 3686416 | tf_op jit(solution)/shard_map/all_gather | solution.py:137
  426.8 17.0 %copy.166 = bf16[64,10,2880]{2,1,0:T(8,128)(2,1)} copy(bf16[64,10,2880]{0,1,2:T(8,128)(2,1)} %all-gather.4.cloned.1.call-done) | data formatting | bytes 7372800 | tf_op jit(solution)/shard_map/all_gather | solution.py:137
  443.8 7.9 %reshape.386 = bf16[640,2880]{1,0:T(8,128)(2,1)} reshape(bf16[64,10,2880]{2,1,0:T(8,128)(2,1)} %copy.166) | data formatting | bytes 7372800 | tf_op jit(solution)/shard_map/reshape | solution.py:144
  451.7 4.3 fusion
  456.8 55.6 %all-gather.6.cloned.1.call-done = bf16[8,180,640]{2,1,0:T(8,128)(2,1)} async-done(((bf16[1,180,640]{2,1,0:T(8,128)(2,1)}), bf16[8,180,640]{2,1,0:T(8,128)(2,1)}) %all-gather.6.cloned.1.call-update) | async-done | bytes 1843216 | tf_op jit(solution)/shard_map/all_gather | solution.py:149
  512.5 1.7 reshape.421
  514.2 3.1 convolution_convert_fusion
  517.3 1.3 copy.167
  518.5 1.1 reshape.387
  519.6 16.0 %all-to-all-start.2 = ((bf16[64,10,360]{2,1,0:T(8,128)(2,1)}), bf16[64,10,360]{2,1,0:T(8,128)(2,1)S(1)}, u32[]{:S(2)}, u32[]{:S(2)}) async-start(bf16[64,10,360]{2,1,0:T(8,128)(2,1)} %reshape.387), calls=%async_computation.2 | async-start | bytes 1572864 | tf_op jit(solution)/shard_map/all_to_all | solution.py:154
  535.9 1.9 gather_fusion.2
  538.5 42.0 %all-to-all-done.2 = bf16[64,10,360]{2,1,0:T(8,128)(2,1)S(1)} async-done(((bf16[64,10,360]{2,1,0:T(8,128)(2,1)}), bf16[64,10,360]{2,1,0:T(8,128)(2,1)S(1)}, u32[]{:S(2)}, u32[]{:S(2)}) %all-to-all-start.2) | async-done | bytes 460832 | tf_op jit(solution)/shard_map/all_to_all | solution.py:154
  580.9 1.0 gather_fusion.1
  582.4 1.6 add_convert_fusion.1
  (94 shorter events, 13.5 us)
Async XLA Ops:
  6.5 40.0 %copy-start = (bf16[256,2880]{0,1:T(8,128)(2,1)S(1)}, bf16[256,2880]{0,1:T(8,128)(2,1)}, u32[]{:S(2)}) copy-start(bf16[256,2880]{0,1:T(8,128)(2,1)} %param.22) | copy-start | bytes 4423684
  6.5 24.1 %copy-start.5 = (f32[4]{0:T(128)S(1)}, f32[4]{0:T(128)}, u32[]{:S(2)}) copy-start(f32[4]{0:T(128)} %param.21) | copy-start | bytes 52
  6.5 24.4 %copy-start.3 = (s32[64,4]{0,1:T(4,128)S(1)}, s32[64,4]{0,1:T(4,128)}, u32[]{:S(2)}) copy-start(s32[64,4]{0,1:T(4,128)} %param.25) | copy-start | bytes 3076
  6.5 37.4 %all-to-all-start = ((bf16[64,8,128]{2,1,0:T(8,128)(2,1)}), bf16[64,8,128]{2,1,0:T(8,128)(2,1)S(1)}, u32[]{:S(2)}, u32[]{:S(2)}) async-start(bf16[64,8,128]{2,1,0:T(8,128)(2,1)} %bitcast.65), calls=%async_computation | async-start | bytes 262144 | tf_op jit(solution)/shard_map/all_to_all | solution.py:87
  25.4 103.4 %all-reduce.3.cloned.1.call-start = ((), (), s32[]{:S(2)}) async-start(), calls=%async_computation.3 | async-start | bytes 1507328 | tf_op jit(solution)/shard_map/psum | solution.py:109
  46.0 1.1 copy-start.2
  48.4 0.9 copy-start.1
  49.3 377.6 %all-gather.4.cloned.1.call-start = ((), (), s32[]{:S(2)}) async-start(), calls=%async_computation.4 | async-start | bytes 13271040 | tf_op jit(solution)/shard_map/all_gather | solution.py:137
  195.5 316.9 %all-gather.6.cloned.1.call-start = ((), (), s32[]{:S(2)}) async-start(), calls=%async_computation.5 | async-start | bytes 2119680 | tf_op jit(solution)/shard_map/all_gather | solution.py:149
  443.8 7.9 %copy-start.6 = (bf16[1,2880,180]{1,2,0:T(8,128)(2,1)S(1)}, bf16[1,2880,180]{1,2,0:T(8,128)(2,1)}, u32[]{:S(2)}) copy-start(bf16[1,2880,180]{1,2,0:T(8,128)(2,1)} %param.28) | copy-start | bytes 3110404
  519.6 60.9 %all-to-all-start.2 = ((bf16[64,10,360]{2,1,0:T(8,128)(2,1)}), bf16[64,10,360]{2,1,0:T(8,128)(2,1)S(1)}, u32[]{:S(2)}, u32[]{:S(2)}) async-start(bf16[64,10,360]{2,1,0:T(8,128)(2,1)} %reshape.387), calls=%async_computation.2 | async-start | bytes 1572864 | tf_op jit(solution)/shard_map/all_to_all | solution.py:154
  535.8 2.5 copy-start.4
Sparse Core Ops, SparseCore 0:
  49.4 79.3 all-reduce.2
  195.7 231.1 all-gather.3
  457.0 55.4 all-gather.5
where the time goes:
time: 592 us; the launch traced here: 591 us
  waiting for transfers between devices  419 us (71%)
  blocking collectives  59.9 us (10%)
  local copies, waits for them, and re-layouts  45.1 us (8%)
  starting transfers between devices  35.2 us (6%)
  between operations  14.2 us (2%)
  matrix products  8.63 us (1%)
  other arithmetic  8.61 us (1%)
    all_gather x1, waiting for transfers between devices, on_device(): lax.all_gather(lax.all_to_all(outgoing, 'group', split_axis=0, concat_axi...  231 us
    psum x1, waiting for transfers between devices, on_device(): hidden_state = lax.psum(partial_sum, 'tp')  78.5 us
    all_to_all x1, blocking collectives, on_device(): lax.all_to_all(outgoing, 'group', split_axis=0, concat_axis=0, tiled=True)  59.9 us
    all_gather x1, waiting for transfers between devices, on_device(): joined = lax.all_gather(active, 'tp', axis=1, tiled=True)  55.6 us
    all_to_all x1, waiting for transfers between devices, on_device(): lax.all_to_all(returned, 'group', split_axis=0, concat_axis=0, tiled=True)  42 us
    all_to_all x1, starting transfers between devices, on_device(): lax.all_to_all(remote_pool.reshape(groups, -1, lane_count), 'group', spli...  18.9 us
    all_gather x1, local copies, waits for them, and re-layouts, on_device(): lax.all_gather(lax.all_to_all(outgoing, 'group', split_axis=0, concat_axi...  17 us
    all_to_all x1, starting transfers between devices, on_device(): lax.all_to_all(returned, 'group', split_axis=0, concat_axis=0, tiled=True)  16 us
  transfers between devices with their start and end apart: 5, of which 5 were waited for; matrix products, arithmetic and copies ran while one was open for 2% of the time, Pallas kernels for 0%

commit v1 on v0

--- a/solution.py
+++ b/solution.py
@@ -106,7 +106,7 @@
     partial_sum = jnp.dot(attended, out_weight, preferred_element_type=jnp.float32)
     own_cols = lax.dynamic_slice_in_dim(partial_sum, start, width, 1) + residual.astype(jnp.float32)
     partial_sum = lax.dynamic_update_slice_in_dim(partial_sum, own_cols, start, 1)
-    hidden_state = lax.psum(partial_sum, "tp")
+    hidden_state = jnp.sum(lax.all_gather(partial_sum, "tp"), axis=0)
     mean_square = jnp.mean(hidden_state * hidden_state, axis=1, keepdims=True)
     own_state = lax.dynamic_slice_in_dim(hidden_state, start, width, 1)
     normed_own = (own_state * lax.rsqrt(mean_square + EPSILON) * own_gain).astype(jnp.bfloat16)

time: 592 us -> 634 us (1.071)
  waiting for transfers between devices: 419 us -> 461 us
    all_gather x0 -> x1, waiting for transfers between devices: none -> 119 us  [on_device(): hidden_state = jnp.sum(lax.all_gather(partial_sum, 'tp'), axis=0)]
    psum x1 -> x0, waiting for transfers between devices: 78.5 us -> none  [on_device(): hidden_state = lax.psum(partial_sum, 'tp')]
where the time goes in v1:
time: 634 us; the launch traced here: 633 us
  waiting for transfers between devices  461 us (73%)
  blocking collectives  60.1 us (9%)
  local copies, waits for them, and re-layouts  44.9 us (7%)
  starting transfers between devices  35.2 us (6%)
  between operations  14.2 us (2%)
  other arithmetic  8.77 us (1%)
  matrix products  8.73 us (1%)
    all_gather x1, waiting for transfers between devices, on_device(): lax.all_gather(lax.all_to_all(outgoing, 'group', split_axis=0, concat_axi...  231 us
    all_gather x1, waiting for transfers between devices, on_device(): hidden_state = jnp.sum(lax.all_gather(partial_sum, 'tp'), axis=0)  119 us
    all_to_all x1, blocking collectives, on_device(): lax.all_to_all(outgoing, 'group', split_axis=0, concat_axis=0, tiled=True)  60.1 us
    all_gather x1, waiting for transfers between devices, on_device(): joined = lax.all_gather(active, 'tp', axis=1, tiled=True)  55.6 us
    all_to_all x1, waiting for transfers between devices, on_device(): lax.all_to_all(returned, 'group', split_axis=0, concat_axis=0, tiled=True)  42 us
    all_to_all x1, starting transfers between devices, on_device(): lax.all_to_all(remote_pool.reshape(groups, -1, lane_count), 'group', spli...  18.9 us
    all_gather x1, local copies, waits for them, and re-layouts, on_device(): lax.all_gather(lax.all_to_all(outgoing, 'group', split_axis=0, concat_axi...  17 us
    all_to_all x1, starting transfers between devices, on_device(): lax.all_to_all(returned, 'group', split_axis=0, concat_axis=0, tiled=True)  16 us
  transfers between devices with their start and end apart: 5, of which 5 were waited for; matrix products, arithmetic and copies ran while one was open for 2% of the time, Pallas kernels for 0%

profile of v1, /device:TPU:2, one launch (start us, length us, event | category | flops | bytes accessed | tf_op | source)
XLA Modules:
  0.0 632.8 jit_solution(13894647310669202136)
XLA Ops:
  6.5 18.9 %all-to-all-start = ((bf16[64,8,128]{2,1,0:T(8,128)(2,1)}), bf16[64,8,128]{2,1,0:T(8,128)(2,1)S(1)}, u32[]{:S(2)}, u32[]{:S(2)}) async-start(bf16[64,8,128]{2,1,0:T(8,128)(2,1)} %bitcast.69), calls=%async_computation | async-start | bytes 262144 | tf_op jit(solution)/shard_map/all_to_all | solution.py:87
  28.0 0.9 reshape.392
  28.9 0.9 copy.144
  31.3 12.6 %all-to-all-done = bf16[64,8,128]{2,1,0:T(8,128)(2,1)S(1)} async-done(((bf16[64,8,128]{2,1,0:T(8,128)(2,1)}), bf16[64,8,128]{2,1,0:T(8,128)(2,1)S(1)}, u32[]{:S(2)}, u32[]{:S(2)}) %all-to-all-start) | async-done | bytes 131104 | tf_op jit(solution)/shard_map/all_to_all | solution.py:87
  47.3 1.1 dynamic_update_slice.4
  48.4 0.9 copy-done.1
  51.4 119.2 %all-gather.5.cloned.1.call-done = f32[8,64,2880]{2,1,0:T(8,128)} async-done(((f32[1,64,2880]{2,1,0:T(8,128)}), f32[8,64,2880]{2,1,0:T(8,128)}) %all-gather.5.cloned.1.call-update) | async-done | bytes 5898256 | tf_op jit(solution)/shard_map/all_gather | solution.py:109
  170.5 3.1 reduce_sum.64
  173.9 2.0 gather_fusion
  176.4 60.1 %all_to_all.15 = bf16[64,10,360]{2,1,0:T(8,128)(2,1)S(1)} all-to-all(bf16[64,10,360]{2,1,0:T(8,128)(2,1)S(1)} %bitcast.62), channel_id=1, replica_groups=mesh['group'=64,'tp'=8] {'group'}, dimensions={0} | all-to-all | bytes 921600 | tf_op jit(solution)/shard_map/all_to_all | solution.py:138
  236.4 2.0 copy.165
  238.7 231.4 %all-gather.7.cloned.1.call-done = bf16[64,10,2880]{0,1,2:T(8,128)(2,1)} async-done(((bf16[64,10,360]{0,1,2:T(8,128)(2,1)}), bf16[64,10,2880]{0,1,2:T(8,128)(2,1)}) %all-gather.7.cloned.1.call-update) | async-done | bytes 3686416 | tf_op jit(solution)/shard_map/all_gather | solution.py:137
  470.0 17.0 %copy.166 = bf16[64,10,2880]{2,1,0:T(8,128)(2,1)} copy(bf16[64,10,2880]{0,1,2:T(8,128)(2,1)} %all-gather.7.cloned.1.call-done) | data formatting | bytes 7372800 | tf_op jit(solution)/shard_map/all_gather | solution.py:137
  487.0 7.8 %reshape.388 = bf16[640,2880]{1,0:T(8,128)(2,1)} reshape(bf16[64,10,2880]{2,1,0:T(8,128)(2,1)} %copy.166) | data formatting | bytes 7372800 | tf_op jit(solution)/shard_map/reshape | solution.py:144
  494.8 4.6 fusion
  499.4 0.9 fusion.14
  500.3 55.6 %all-gather.9.cloned.1.call-done = bf16[8,180,640]{2,1,0:T(8,128)(2,1)} async-done(((bf16[1,180,640]{2,1,0:T(8,128)(2,1)}), bf16[8,180,640]{2,1,0:T(8,128)(2,1)}) %all-gather.9.cloned.1.call-update) | async-done | bytes 1843216 | tf_op jit(solution)/shard_map/all_gather | solution.py:149
  555.9 2.6 reshape.423
  558.5 2.9 convolution_convert_fusion
  561.7 1.1 reshape.389
  562.8 16.0 %all-to-all-start.2 = ((bf16[64,10,360]{2,1,0:T(8,128)(2,1)}), bf16[64,10,360]{2,1,0:T(8,128)(2,1)S(1)}, u32[]{:S(2)}, u32[]{:S(2)}) async-start(bf16[64,10,360]{2,1,0:T(8,128)(2,1)} %reshape.389), calls=%async_computation.2 | async-start | bytes 1572864 | tf_op jit(solution)/shard_map/all_to_all | solution.py:154
  579.0 1.9 gather_fusion.2
  581.6 42.0 %all-to-all-done.2 = bf16[64,10,360]{2,1,0:T(8,128)(2,1)S(1)} async-done(((bf16[64,10,360]{2,1,0:T(8,128)(2,1)}), bf16[64,10,360]{2,1,0:T(8,128)(2,1)S(1)}, u32[]{:S(2)}, u32[]{:S(2)}) %all-to-all-start.2) | async-done | bytes 460832 | tf_op jit(solution)/shard_map/all_to_all | solution.py:154
  624.0 1.0 gather_fusion.1
  (93 shorter events, 12.2 us)
Async XLA Ops:
  6.5 40.0 %copy-start = (bf16[256,2880]{0,1:T(8,128)(2,1)S(1)}, bf16[256,2880]{0,1:T(8,128)(2,1)}, u32[]{:S(2)}) copy-start(bf16[256,2880]{0,1:T(8,128)(2,1)} %param.22) | copy-start | bytes 4423684
  6.5 24.3 %copy-start.5 = (f32[4]{0:T(128)S(1)}, f32[4]{0:T(128)}, u32[]{:S(2)}) copy-start(f32[4]{0:T(128)} %param.21) | copy-start | bytes 52
  6.5 37.4 %all-to-all-start = ((bf16[64,8,128]{2,1,0:T(8,128)(2,1)}), bf16[64,8,128]{2,1,0:T(8,128)(2,1)S(1)}, u32[]{:S(2)}, u32[]{:S(2)}) async-start(bf16[64,8,128]{2,1,0:T(8,128)(2,1)} %bitcast.69), calls=%async_computation | async-start | bytes 262144 | tf_op jit(solution)/shard_map/all_to_all | solution.py:87
  25.4 145.1 %all-gather.5.cloned.1.call-start = ((), (), s32[]{:S(2)}) async-start(), calls=%async_computation.3 | async-start | bytes 6782976 | tf_op jit(solution)/shard_map/all_gather | solution.py:109
  46.0 1.1 copy-start.2
  46.3 3.0 copy-start.3
  48.4 0.9 copy-start.1
  49.3 420.8 %all-gather.7.cloned.1.call-start = ((), (), s32[]{:S(2)}) async-start(), calls=%async_computation.4 | async-start | bytes 13271040 | tf_op jit(solution)/shard_map/all_gather | solution.py:137
  238.4 317.5 %all-gather.9.cloned.1.call-start = ((), (), s32[]{:S(2)}) async-start(), calls=%async_computation.5 | async-start | bytes 2119680 | tf_op jit(solution)/shard_map/all_gather | solution.py:149
  562.8 60.9 %all-to-all-start.2 = ((bf16[64,10,360]{2,1,0:T(8,128)(2,1)}), bf16[64,10,360]{2,1,0:T(8,128)(2,1)S(1)}, u32[]{:S(2)}, u32[]{:S(2)}) async-start(bf16[64,10,360]{2,1,0:T(8,128)(2,1)} %reshape.389), calls=%async_computation.2 | async-start | bytes 1572864 | tf_op jit(solution)/shard_map/all_to_all | solution.py:154
  579.0 2.5 copy-start.4
Sparse Core Ops, SparseCore 0:
  49.4 121.1 all-gather.4
  238.6 231.4 all-gather.6
  500.4 55.4 all-gather.8
